TPU v7x, 128 devices: a whole 4x4x4 slice. The times are simulated.
128 devices in a mesh: gx: 8 (over z, y_lo), gy: 4 (over y_hi, core), gz: 4 (over x).
Axes of the slice: x: 4, y: 4 (y_hi: 2, y_lo: 2; y = y_hi * 2 + y_lo), z: 4, core: 2. Of those that a mesh axis runs over, the one named last changes fastest.
Arguments:
- residual: float32 [64, 3, 32, 16, 512], P(None, None, 'gx', 'gy', 'gz'), may hold values from -8 to 8
- interface_scaling: float32 [3, 32, 16, 512], P(None, 'gx', 'gy', 'gz'), may hold values from 0.3 to 0.7
- primal_basis: bfloat16 [8, 4, 4, 128, 6144], P('gx', 'gy', 'gz'), may hold values from -0.078125 to 0.078125
- primal_index: int32 [8, 4, 4, 128], P('gx', 'gy', 'gz'), may hold values from 0 to 1023
- coarse_inverse: float32 [8192, 1024], P('gx'), may hold values from -2 to 2
- schur_tiles: bfloat16 [8, 4, 4, 48, 6, 128, 128], P('gx', 'gy', 'gz'), may hold values from -0.3125 to 0.3125
- tile_cols: int32 [8, 4, 4, 48, 6], P('gx', 'gy', 'gz'), may hold values from 0 to 47
- tile_count: int32 [8, 4, 4, 48], P('gx', 'gy', 'gz'), may hold values from 1 to 6, as said below
- region_id: int32 [8, 4, 4], P('gx', 'gy', 'gz'), may hold values from 0 to 7
- region_viscosity: float32 [8], replicated, may hold values from 0.5 to 4
Outputs:
- preconditioned: float32 [64, 3, 32, 16, 512], P(None, None, 'gx', 'gy', 'gz')
Inputs may be any that keep to these rules, and one draw needn't show every extreme that they name: Only the first tile_count slots of a block row carry tiles; some block row has all 6 in every draw.
All inputs are finite; a program needn't handle non-finite values.
Results may differ from a plain program's by a relative error of at most 0.004.
Values sent between devices are 32-bit elements; how exact they have to be, the bound alone decides.
A program may use at most 128 MiB of HBM per device.

v0:
```python
import math

import jax
import jax.numpy as jnp
from jax import lax
from jax.sharding import PartitionSpec as P


def padded_2(cells, sides, width):
    for axis, dim in sides:
        count = lax.axis_size(axis)
        ends = count - 1
        head = lax.slice_in_dim(cells, 0, width, axis=dim)
        tail = lax.slice_in_dim(cells, cells.shape[dim] - width, cells.shape[dim], axis=dim)
        cells = jnp.concatenate(
            [
                lax.ppermute(tail, axis, [(i, (i + 1) % count) for i in range(ends)]),
                cells,
                lax.ppermute(head, axis, [((i + 1) % count, i) for i in range(ends)]),
            ],
            axis=dim,
        )
    return cells


def face_terms(grid_field, padded, axis_id):
    extent = grid_field.shape[axis_id]
    below = lax.slice_in_dim(padded, 0, extent, axis=axis_id)
    above = lax.slice_in_dim(padded, 2, extent + 2, axis=axis_id)
    positions = jnp.arange(extent)
    mask_shape = [extent if dim_id == axis_id else 1 for dim_id in range(5)]
    at_start = (positions == 0).reshape(mask_shape)
    at_end = (positions == extent - 1).reshape(mask_shape)
    return jnp.where(at_start, below, 0.0) + jnp.where(at_end, above, 0.0)


def interface_sum(grid_field):
    summed = grid_field
    padded = padded_2(grid_field, (("gx", 2), ("gy", 3), ("gz", 4)), 1)
    for axis_id in (2, 3, 4):
        trimmed = padded
        for other_axis in (2, 3, 4):
            if other_axis != axis_id:
                trimmed = lax.slice_in_dim(
                    trimmed, 1, grid_field.shape[other_axis] + 1, axis=other_axis
                )
        summed = summed + face_terms(grid_field, trimmed, axis_id)
    return summed


def per_device(
    residual,
    interface_scaling,
    primal_basis,
    primal_index,
    coarse_inverse,
    schur_tiles,
    tile_cols,
    tile_count,
    region_id,
    region_viscosity,
):
    highest = lax.Precision.HIGHEST
    rhs_count = residual.shape[0]
    cells_z = residual.shape[4]
    weighted = (interface_scaling[None] * interface_sum(residual)).astype(jnp.bfloat16)
    flat_rows = weighted.reshape(rhs_count, -1)
    basis = primal_basis[0, 0, 0]
    indices = primal_index[0, 0, 0]
    coarse_slots = coarse_inverse.shape[1]
    one_hot = (indices[:, None] == jnp.arange(coarse_slots)[None, :]).astype(jnp.float32)
    coarse_part = lax.dot_general(
        flat_rows, basis, (((1,), (1,)), ((), ())), preferred_element_type=jnp.float32
    )
    local_coarse = jnp.dot(coarse_part, one_hot, precision=highest)
    coarse_residual = lax.psum(local_coarse, ("gy", "gz"))
    coarse_solution = lax.dot_general(
        coarse_residual, coarse_inverse, (((1,), (1,)), ((), ())), precision=highest
    )
    picked = jnp.dot(coarse_solution, one_hot.T, precision=highest).astype(jnp.bfloat16)
    scale_factor = math.sqrt(flat_rows.shape[1] / basis.shape[0])
    coarse_fix = jnp.dot(picked, basis, preferred_element_type=jnp.float32) * scale_factor
    blocks = flat_rows.reshape(rhs_count, -1, cells_z)
    tiles = schur_tiles[0, 0, 0]
    columns = tile_cols[0, 0, 0]
    live = tile_count[0, 0, 0]

    def add_slot(slot, schur_sum):
        tile_now = lax.dynamic_index_in_dim(tiles, slot, 1, keepdims=False)
        cols_now = lax.dynamic_index_in_dim(columns, slot, 1, keepdims=False)
        chosen = jnp.take(blocks, cols_now, axis=1)
        product = jnp.einsum("bij,sbj->sbi", tile_now, chosen, preferred_element_type=jnp.float32)
        return schur_sum + jnp.where((live > slot)[None, :, None], product, 0.0)

    schur_sum = lax.fori_loop(0, jnp.max(live), add_slot, jnp.zeros(blocks.shape, jnp.float32))
    region_now = region_id.reshape(())
    inverse_visc = jnp.sum(
        jnp.where(jnp.arange(region_viscosity.shape[0]) == region_now, 1.0 / region_viscosity, 0.0)
    )
    correction = coarse_fix + schur_sum.reshape(rhs_count, -1) * inverse_visc
    correction = correction.reshape(residual.shape)
    return interface_scaling[None] * interface_sum(correction)


def solution(mesh):
    in_specs = (
        P(None, None, "gx", "gy", "gz"),
        P(None, "gx", "gy", "gz"),
        P("gx", "gy", "gz", None, None),
        P("gx", "gy", "gz", None),
        P("gx", None),
        P("gx", "gy", "gz", None, None, None, None),
        P("gx", "gy", "gz", None, None),
        P("gx", "gy", "gz", None),
        P("gx", "gy", "gz"),
        P(),
    )
    out_specs = P(None, None, "gx", "gy", "gz")
    return jax.shard_map(
        per_device, mesh=mesh, in_specs=in_specs, out_specs=out_specs, check_vma=False
    )
```

profile of v0, /device:TPU:97, one launch (start us, length us, event | category | flops | bytes accessed | tf_op | source)
XLA Modules:
  0.0 315.5 jit_solution(6079211764691938750)
XLA Ops:
  6.5 2.0 copy.67
  8.7 3.5 %collective-permute-start = (f32[64,3,1,4,128]{4,0,3,2,1:T(8,128)S(1)}, f32[64,3,1,4,128]{4,0,3,2,1:T(8,128)S(1)}, u32[]{:S(2)}, u32[]{:S(2)}) collective-permute-start(f32[64,3,1,4,128]{4,0,3,2,1:T(8,128)S(1)} %get-tuple-element.85), channel_id=1, source_target_pairs={{0,16},{16,32},{32,48},{48,64},{64,80},{80,96},{96,112},{1,17},{17... | collective-permute-start | bytes 1179656 | tf_op jit(solution)/shard_map/ppermute | solution.py:17
  12.2 3.0 collective-permute-start.1
  15.1 6.6 %collective-permute-done = f32[64,3,1,4,128]{4,0,3,2,1:T(8,128)S(1)} collective-permute-done((f32[64,3,1,4,128]{4,0,3,2,1:T(8,128)S(1)}, f32[64,3,1,4,128]{4,0,3,2,1:T(8,128)S(1)}, u32[]{:S(2)}, u32[]{:S(2)}) %collective-permute-start) | collective-permute-done | bytes 393248 | tf_op jit(solution)/shard_map/ppermute | solution.py:17
  23.0 5.3 %collective-permute-done.1 = f32[64,3,1,4,128]{4,0,3,2,1:T(8,128)S(1)} collective-permute-done((f32[64,3,1,4,128]{4,0,3,2,1:T(8,128)S(1)}, f32[64,3,1,4,128]{4,0,3,2,1:T(8,128)S(1)}, u32[]{:S(2)}, u32[]{:S(2)}) %collective-permute-start.1) | collective-permute-done | bytes 393248 | tf_op jit(solution)/shard_map/ppermute | solution.py:19
  29.1 5.9 %collective-permute-start.2 = (f32[64,3,6,1,128]{4,0,3,2,1:T(8,128)S(1)}, f32[64,3,6,1,128]{4,0,3,2,1:T(8,128)S(1)}, u32[]{:S(2)}, u32[]{:S(2)}) collective-permute-start(f32[64,3,6,1,128]{4,0,3,2,1:T(8,128)S(1)} %get-tuple-element.80), channel_id=1, source_target_pairs={{0,4},{4,8},{8,12},{1,5},{5,9},{9,13},{2,6},{6,10},{10,14},{3,7},{... | collective-permute-start | bytes 1769480 | tf_op jit(solution)/shard_map/ppermute | solution.py:17
  35.1 1.9 collective-permute-start.3
  38.8 3.0 collective-permute-done.2
  41.9 5.9 %collective-permute-done.3 = f32[64,3,6,1,128]{4,0,3,2,1:T(8,128)S(1)} collective-permute-done((f32[64,3,6,1,128]{4,0,3,2,1:T(8,128)S(1)}, f32[64,3,6,1,128]{4,0,3,2,1:T(8,128)S(1)}, u32[]{:S(2)}, u32[]{:S(2)}) %collective-permute-start.3) | collective-permute-done | bytes 589856 | tf_op jit(solution)/shard_map/ppermute | solution.py:19
  48.2 4.1 %fusion.47 = (f32[64,3,6,6,1]{4,0,3,2,1:T(8,128)}, f32[64,3,6,6,1]{4,0,3,2,1:T(8,128)}) fusion(f32[64,3,6,6,128]{4,0,3,2,1:T(8,128)S(1)} %pad_maximum_fusion), kind=kLoop, calls=%fused_computation.90 | loop fusion | bytes 110592 | tf_op jit(solution)/shard_map/slice | solution.py:14
  52.2 2.6 copy.69
  54.9 3.1 collective-permute-start.4
  58.0 2.7 copy.71
  60.7 1.3 collective-permute-start.5
  62.0 11.6 %copy.94 = bf16[1,1,1,48,6,128,128]{6,5,3,4,2,1,0:T(8,128)(2,1)} copy(bf16[1,1,1,48,6,128,128]{6,5,4,3,2,1,0:T(8,128)(2,1)} %param.17) | data formatting | bytes 18874368 | tf_op args[5]
  74.3 2.4 copy.70
  76.7 2.5 copy.72
  79.2 6.3 %fusion.29 = bf16[64,3,4,4,128]{4,0,3,2,1:T(8,128)(2,1)S(1)} fusion(f32[64,3,6,6,1]{4,0,3,2,1:T(8,128)} %copy.72, f32[64,3,6,1,128]{4,0,3,2,1:T(8,128)S(1)} %collective-permute-done.3, f32[64,3,6,4,128]{4,0,3,2,1:T(8,128)} %copy-done.3, f32[64,3,6,1,128]{4,0,3,2,1:T(8,128)S(1)} %collective-permute-done.2, f32[64,3,6,6,1]{4,0,3,2,1:T(8,128)} %copy.70, ...), kind=kLoop, calls=%fused_computation.48 | loop fusion | flops 9437184 | bytes 6764808 | tf_op jit(solution)/shard_map/convert_element_type | solution.py:66
  86.2 1.5 reshape.57
  87.7 1.8 fusion.40
  89.5 1.1 fusion.42
  90.6 1.3 broadcast_in_dim.126
  92.0 12.1 %while.10 = (s32[]{:T(128)}, f32[64,48,128]{2,0,1:T(8,128)}, s32[]{:T(128)}, s32[48]{0:T(128)S(1)}, s32[48,6]{0,1:T(8,128)S(1)}, /*index=5*/bf16[64,48,128]{2,0,...) while((s32[]{:T(128)}, f32[64,48,128]{2,0,1:T(8,128)}, s32[]{:T(128)}, ...), condition=%wide.region_3.4_spmd, body=%wide.region_2.3_spmd.sunk | while | flops 101844304 | bytes 7083283 | solution.py:95
  93.4 4.2 %bitcast_add_fusion.2 = f32[64,48,128]{2,0,1:T(8,128)} fusion(f32[64,48,128]{2,0,1:T(8,128)} %get-tuple-element.149, bf16[48,6,128,128]{3,2,0,1:T(8,128)(2,1)} %get-tuple-element.164, s32[]{:T(128)S(6)} %select_n.158, bf16[48,64,128]{2,1,0:T(8,128)(2,1)S(1)} %gather_fusion, pred[48]{0:T(512)(128)(4,1)S(1)} %get-tuple-element.137, ...), kind=kOutput, calls=%fused_computation.1.clone.1 | convolution fusion | flops 101842944 | bytes 5505124 | tf_op jit(solution)/shard_map/while/body/bij,sbj->sbi/dot_general | solution.py:92
  99.0 4.2 %bitcast_add_fusion.2 = f32[64,48,128]{2,0,1:T(8,128)} fusion(f32[64,48,128]{2,0,1:T(8,128)} %get-tuple-element.149, bf16[48,6,128,128]{3,2,0,1:T(8,128)(2,1)} %get-tuple-element.164, s32[]{:T(128)S(6)} %select_n.158, bf16[48,64,128]{2,1,0:T(8,128)(2,1)S(1)} %gather_fusion, pred[48]{0:T(512)(128)(4,1)S(1)} %get-tuple-element.137, ...), kind=kOutput, calls=%fused_computation.1.clone.1 | convolution fusion | flops 101842944 | bytes 5505124 | tf_op jit(solution)/shard_map/while/body/bij,sbj->sbi/dot_general | solution.py:92
  104.1 122.9 %all-reduce.2.cloned.1.call-done = f32[64,1024]{1,0:T(8,128)} async-done(((f32[64,1024]{1,0:T(8,128)}), f32[64,1024]{1,0:T(8,128)}) %all-reduce.2.cloned.1.call-update) | async-done | bytes 262160 | tf_op jit(solution)/shard_map/psum | solution.py:76
  226.9 6.3 %fusion.52 = f32[64,1024]{1,0:T(8,128)S(1)} fusion(f32[64,1024]{1,0:T(8,128)} %all-reduce.2.cloned.1.call-done, f32[1024,1024]{1,0:T(8,128)} %param.16), kind=kOutput, calls=%fused_computation.95 | convolution fusion | flops 805306368 | bytes 4718592 | tf_op jit(solution)/shard_map/dot_general | solution.py:77
  233.8 2.1 fusion.11
  235.9 2.4 reshape.59
  238.9 2.5 collective-permute-start.6
  241.4 3.6 %collective-permute-start.7 = (f32[64,3,1,4,128]{4,0,3,2,1:T(8,128)S(1)}, f32[64,3,1,4,128]{4,0,3,2,1:T(8,128)S(1)}, u32[]{:S(2)}, u32[]{:S(2)}) collective-permute-start(f32[64,3,1,4,128]{4,0,3,2,1:T(8,128)S(1)} %get-tuple-element.82), channel_id=1, source_target_pairs={{16,0},{32,16},{48,32},{64,48},{80,64},{96,80},{112,96},{17,1},{33... | collective-permute-start | bytes 1179656 | tf_op jit(solution)/shard_map/ppermute | solution.py:19
  245.1 3.2 %collective-permute-done.6 = f32[64,3,1,4,128]{4,0,3,2,1:T(8,128)S(1)} collective-permute-done((f32[64,3,1,4,128]{4,0,3,2,1:T(8,128)S(1)}, f32[64,3,1,4,128]{4,0,3,2,1:T(8,128)S(1)}, u32[]{:S(2)}, u32[]{:S(2)}) %collective-permute-start.6) | collective-permute-done | bytes 393248 | tf_op jit(solution)/shard_map/ppermute | solution.py:17
  248.8 5.4 %collective-permute-done.7 = f32[64,3,1,4,128]{4,0,3,2,1:T(8,128)S(1)} collective-permute-done((f32[64,3,1,4,128]{4,0,3,2,1:T(8,128)S(1)}, f32[64,3,1,4,128]{4,0,3,2,1:T(8,128)S(1)}, u32[]{:S(2)}, u32[]{:S(2)}) %collective-permute-start.7) | collective-permute-done | bytes 393248 | tf_op jit(solution)/shard_map/ppermute | solution.py:19
  255.0 9.2 %collective-permute-start.8 = (f32[64,3,6,1,128]{4,0,3,2,1:T(8,128)S(1)}, f32[64,3,6,1,128]{4,0,3,2,1:T(8,128)S(1)}, u32[]{:S(2)}, u32[]{:S(2)}) collective-permute-start(f32[64,3,6,1,128]{4,0,3,2,1:T(8,128)S(1)} %get-tuple-element.78), channel_id=1, source_target_pairs={{0,4},{4,8},{8,12},{1,5},{5,9},{9,13},{2,6},{6,10},{10,14},{3,7},{... | collective-permute-start | bytes 1769480 | tf_op jit(solution)/shard_map/ppermute | solution.py:17
  264.1 1.9 collective-permute-start.9
  266.1 4.9 %collective-permute-done.8 = f32[64,3,6,1,128]{4,0,3,2,1:T(8,128)S(1)} collective-permute-done((f32[64,3,6,1,128]{4,0,3,2,1:T(8,128)S(1)}, f32[64,3,6,1,128]{4,0,3,2,1:T(8,128)S(1)}, u32[]{:S(2)}, u32[]{:S(2)}) %collective-permute-start.8) | collective-permute-done | bytes 589856 | tf_op jit(solution)/shard_map/ppermute | solution.py:17
  271.0 5.9 %collective-permute-done.9 = f32[64,3,6,1,128]{4,0,3,2,1:T(8,128)S(1)} collective-permute-done((f32[64,3,6,1,128]{4,0,3,2,1:T(8,128)S(1)}, f32[64,3,6,1,128]{4,0,3,2,1:T(8,128)S(1)}, u32[]{:S(2)}, u32[]{:S(2)}) %collective-permute-start.9) | collective-permute-done | bytes 589856 | tf_op jit(solution)/shard_map/ppermute | solution.py:19
  276.9 0.8 copy-done.9
  277.9 4.0 %fusion.46 = (f32[64,3,6,6,1]{4,0,3,2,1:T(8,128)}, f32[64,3,6,6,1]{4,0,3,2,1:T(8,128)}) fusion(f32[64,3,6,6,128]{4,0,3,2,1:T(8,128)S(1)} %pad_maximum_fusion.1), kind=kLoop, calls=%fused_computation.89 | loop fusion | bytes 110592 | tf_op jit(solution)/shard_map/slice | solution.py:14
  281.9 3.0 copy.82
  284.9 4.2 %collective-permute-start.10 = (f32[64,3,6,6,1]{0,3,4,2,1:T(8,128)S(1)}, f32[64,3,6,6,1]{0,3,4,2,1:T(8,128)S(1)}, u32[]{:S(2)}, u32[]{:S(2)}) collective-permute-start(f32[64,3,6,6,1]{0,3,4,2,1:T(8,128)S(1)} %copy.82), channel_id=1, source_target_pairs={{0,1},{1,2},{2,3},{4,5},{5,6},{6,7},{8,9},{9,10},{10,11},{12,13},{... | collective-permute-start | bytes 82952 | tf_op jit(solution)/shard_map/ppermute | solution.py:17
  289.2 3.6 %copy.84 = f32[64,3,6,6,1]{0,3,4,2,1:T(8,128)} copy(f32[64,3,6,6,1]{4,0,3,2,1:T(8,128)} %get-tuple-element.75) | data formatting | bytes 55296 | tf_op jit(solution)/shard_map/slice | solution.py:13
  292.8 1.5 collective-permute-start.11
  294.3 2.5 copy.83
  296.8 1.4 collective-permute-done.11
  298.2 3.2 %copy.85 = f32[64,3,6,6,1]{4,0,3,2,1:T(8,128)} copy(f32[64,3,6,6,1]{0,3,4,2,1:T(8,128)} %collective-permute-done.11) | data formatting | bytes 55296 | tf_op jit(solution)/shard_map/ppermute | solution.py:19
  301.4 5.1 %fusion.15 = f32[64,3,4,4,128]{4,0,3,2,1:T(8,128)S(1)} fusion(f32[64,3,6,6,1]{4,0,3,2,1:T(8,128)} %copy.85, f32[64,3,6,1,128]{4,0,3,2,1:T(8,128)} %copy-done.9, f32[64,3,6,4,128]{4,0,3,2,1:T(8,128)} %copy-done.2, f32[64,3,6,1,128]{4,0,3,2,1:T(8,128)} %copy-done.8, f32[64,3,6,6,1]{4,0,3,2,1:T(8,128)} %copy.83, f32[64,3,4,4,128]{4,0,3,2,1:T(8,128)S(1)} %copy-done.6, ...), kind=kLoop, calls=%fused_computation.24 | loop fusion | flops 9043968 | bytes 7551240 | tf_op jit(solution)/shard_map/mul | solution.py:102
  306.5 2.2 copy.86
  (70 shorter events, 9.0 us)
Async XLA Ops:
  6.5 81.1 %copy-start = (bf16[1,1,1,128,6144]{4,3,2,1,0:T(8,128)(2,1)S(1)}, bf16[1,1,1,128,6144]{4,3,2,1,0:T(8,128)(2,1)}, u32[]{:S(2)}) copy-start(bf16[1,1,1,128,6144]{4,3,2,1,0:T(8,128)(2,1)} %param.14) | copy-start | bytes 4718596
  6.5 220.4 %all-reduce.2.cloned.1.call-start = ((), (), s32[]{:S(2)}) async-start(), calls=%async_computation | async-start | bytes 524288 | tf_op jit(solution)/shard_map/psum | solution.py:76
  8.6 14.4 %copy-start.4 = (f32[64,3,4,4,128]{4,0,3,2,1:T(8,128)}, f32[64,3,4,4,128]{4,0,3,2,1:T(8,128)S(1)}, u32[]{:S(2)}) copy-start(f32[64,3,4,4,128]{4,0,3,2,1:T(8,128)S(1)} %copy.67) | copy-start | bytes 4718596
  8.6 13.9 %copy-start.7 = (f32[64,3,4,4,128]{4,3,2,1,0:T(4,128)S(1)}, f32[64,3,4,4,128]{4,3,2,1,0:T(4,128)}, u32[]{:S(2)}) copy-start(f32[64,3,4,4,128]{4,3,2,1,0:T(4,128)} %param.12) | copy-start | bytes 4718596
  8.7 13.0 %collective-permute-start = (f32[64,3,1,4,128]{4,0,3,2,1:T(8,128)S(1)}, f32[64,3,1,4,128]{4,0,3,2,1:T(8,128)S(1)}, u32[]{:S(2)}, u32[]{:S(2)}) collective-permute-start(f32[64,3,1,4,128]{4,0,3,2,1:T(8,128)S(1)} %get-tuple-element.85), channel_id=1, source_target_pairs={{0,16},{16,32},{32,48},{48,64},{64,80},{80,96},{96,112},{1,17},{17... | collective-permute-start | bytes 1179656 | tf_op jit(solution)/shard_map/ppermute | solution.py:17
  12.2 16.2 %collective-permute-start.1 = (f32[64,3,1,4,128]{4,0,3,2,1:T(8,128)S(1)}, f32[64,3,1,4,128]{4,0,3,2,1:T(8,128)S(1)}, u32[]{:S(2)}, u32[]{:S(2)}) collective-permute-start(f32[64,3,1,4,128]{4,0,3,2,1:T(8,128)S(1)} %get-tuple-element.84), channel_id=1, source_target_pairs={{16,0},{32,16},{48,32},{64,48},{80,64},{96,80},{112,96},{17,1},{33... | collective-permute-start | bytes 1179656 | tf_op jit(solution)/shard_map/ppermute | solution.py:19
  21.7 0.8 copy-start.10
  23.0 15.2 %copy-start.16 = (f32[8]{0:T(128)S(1)}, f32[8]{0:T(128)}, u32[]{:S(2)}) copy-start(f32[8]{0:T(128)} %param.21) | copy-start | bytes 100
  28.3 0.8 copy-start.11
  28.4 19.4 %copy-start.3 = (f32[64,3,6,4,128]{4,0,3,2,1:T(8,128)}, f32[64,3,6,4,128]{4,0,3,2,1:T(8,128)S(1)}, u32[]{:S(2)}) copy-start(f32[64,3,6,4,128]{4,0,3,2,1:T(8,128)S(1)} %constant_dynamic-update-slice_fusion) | copy-start | bytes 7077892
  29.1 12.8 %collective-permute-start.2 = (f32[64,3,6,1,128]{4,0,3,2,1:T(8,128)S(1)}, f32[64,3,6,1,128]{4,0,3,2,1:T(8,128)S(1)}, u32[]{:S(2)}, u32[]{:S(2)}) collective-permute-start(f32[64,3,6,1,128]{4,0,3,2,1:T(8,128)S(1)} %get-tuple-element.80), channel_id=1, source_target_pairs={{0,4},{4,8},{8,12},{1,5},{5,9},{9,13},{2,6},{6,10},{10,14},{3,7},{... | collective-permute-start | bytes 1769480 | tf_op jit(solution)/shard_map/ppermute | solution.py:17
  35.1 12.7 %collective-permute-start.3 = (f32[64,3,6,1,128]{4,0,3,2,1:T(8,128)S(1)}, f32[64,3,6,1,128]{4,0,3,2,1:T(8,128)S(1)}, u32[]{:S(2)}, u32[]{:S(2)}) collective-permute-start(f32[64,3,6,1,128]{4,0,3,2,1:T(8,128)S(1)} %get-tuple-element.81), channel_id=1, source_target_pairs={{4,0},{8,4},{12,8},{5,1},{9,5},{13,9},{6,2},{10,6},{14,10},{7,3},{... | collective-permute-start | bytes 1769480 | tf_op jit(solution)/shard_map/ppermute | solution.py:19
  54.9 19.4 %collective-permute-start.4 = (f32[64,3,6,6,1]{0,4,3,2,1:T(1,128)S(1)}, f32[64,3,6,6,1]{0,4,3,2,1:T(1,128)S(1)}, u32[]{:S(2)}, u32[]{:S(2)}) collective-permute-start(f32[64,3,6,6,1]{0,4,3,2,1:T(1,128)S(1)} %copy.69), channel_id=1, source_target_pairs={{0,1},{1,2},{2,3},{4,5},{5,6},{6,7},{8,9},{9,10},{10,11},{12,13},{... | collective-permute-start | bytes 82952 | tf_op jit(solution)/shard_map/ppermute | solution.py:17
  60.7 16.1 %collective-permute-start.5 = (f32[64,3,6,6,1]{0,4,3,2,1:T(1,128)S(1)}, f32[64,3,6,6,1]{0,4,3,2,1:T(1,128)S(1)}, u32[]{:S(2)}, u32[]{:S(2)}) collective-permute-start(f32[64,3,6,6,1]{0,4,3,2,1:T(1,128)S(1)} %copy.71), channel_id=1, source_target_pairs={{1,0},{2,1},{3,2},{5,4},{6,5},{7,6},{9,8},{10,9},{11,10},{13,12},{... | collective-permute-start | bytes 82952 | tf_op jit(solution)/shard_map/ppermute | solution.py:19
  62.0 11.6 %copy-start.13 = (s32[1,1,1,48,6]{3,2,4,1,0:T(1,128)S(1)}, s32[1,1,1,48,6]{3,2,4,1,0:T(1,128)}, u32[]{:S(2)}) copy-start(s32[1,1,1,48,6]{3,2,4,1,0:T(1,128)} %param.18) | copy-start | bytes 3460
  62.0 11.6 %copy-start.17 = (s32[1,1,1,48]{3,2,1,0:T(1,128)S(1)}, s32[1,1,1,48]{3,2,1,0:T(1,128)}, u32[]{:S(2)}) copy-start(s32[1,1,1,48]{3,2,1,0:T(1,128)} %param.19) | copy-start | bytes 580
  87.7 1.8 copy-start.14
  89.5 2.5 copy-start.18
  104.0 129.7 %copy-start.1 = (f32[64,48,128]{2,0,1:T(8,128)S(1)}, f32[64,48,128]{2,0,1:T(8,128)}, u32[]{:S(2)}) copy-start(f32[64,48,128]{2,0,1:T(8,128)} %get-tuple-element.43) | copy-start | bytes 4718596
  238.8 10.0 %copy-start.5 = (f32[64,3,4,4,128]{4,0,3,2,1:T(8,128)}, f32[64,3,4,4,128]{4,0,3,2,1:T(8,128)S(1)}, u32[]{:S(2)}) copy-start(f32[64,3,4,4,128]{4,0,3,2,1:T(8,128)S(1)} %copy.80) | copy-start | bytes 4718596
  238.9 9.4 %collective-permute-start.6 = (f32[64,3,1,4,128]{4,0,3,2,1:T(8,128)S(1)}, f32[64,3,1,4,128]{4,0,3,2,1:T(8,128)S(1)}, u32[]{:S(2)}, u32[]{:S(2)}) collective-permute-start(f32[64,3,1,4,128]{4,0,3,2,1:T(8,128)S(1)} %get-tuple-element.83), channel_id=1, source_target_pairs={{0,16},{16,32},{32,48},{48,64},{64,80},{80,96},{96,112},{1,17},{17... | collective-permute-start | bytes 1179656 | tf_op jit(solution)/shard_map/ppermute | solution.py:17
  241.4 12.8 %collective-permute-start.7 = (f32[64,3,1,4,128]{4,0,3,2,1:T(8,128)S(1)}, f32[64,3,1,4,128]{4,0,3,2,1:T(8,128)S(1)}, u32[]{:S(2)}, u32[]{:S(2)}) collective-permute-start(f32[64,3,1,4,128]{4,0,3,2,1:T(8,128)S(1)} %get-tuple-element.82), channel_id=1, source_target_pairs={{16,0},{32,16},{48,32},{64,48},{80,64},{96,80},{112,96},{17,1},{33... | collective-permute-start | bytes 1179656 | tf_op jit(solution)/shard_map/ppermute | solution.py:19
  254.2 0.7 copy-start.12
  254.3 22.6 %copy-start.2 = (f32[64,3,6,4,128]{4,0,3,2,1:T(8,128)}, f32[64,3,6,4,128]{4,0,3,2,1:T(8,128)S(1)}, u32[]{:S(2)}) copy-start(f32[64,3,6,4,128]{4,0,3,2,1:T(8,128)S(1)} %constant_dynamic-update-slice_fusion.3) | copy-start | bytes 7077892
  255.0 16.0 %collective-permute-start.8 = (f32[64,3,6,1,128]{4,0,3,2,1:T(8,128)S(1)}, f32[64,3,6,1,128]{4,0,3,2,1:T(8,128)S(1)}, u32[]{:S(2)}, u32[]{:S(2)}) collective-permute-start(f32[64,3,6,1,128]{4,0,3,2,1:T(8,128)S(1)} %get-tuple-element.78), channel_id=1, source_target_pairs={{0,4},{4,8},{8,12},{1,5},{5,9},{9,13},{2,6},{6,10},{10,14},{3,7},{... | collective-permute-start | bytes 1769480 | tf_op jit(solution)/shard_map/ppermute | solution.py:17
  264.1 12.7 %collective-permute-start.9 = (f32[64,3,6,1,128]{4,0,3,2,1:T(8,128)S(1)}, f32[64,3,6,1,128]{4,0,3,2,1:T(8,128)S(1)}, u32[]{:S(2)}, u32[]{:S(2)}) collective-permute-start(f32[64,3,6,1,128]{4,0,3,2,1:T(8,128)S(1)} %get-tuple-element.79), channel_id=1, source_target_pairs={{4,0},{8,4},{12,8},{5,1},{9,5},{13,9},{6,2},{10,6},{14,10},{7,3},{... | collective-permute-start | bytes 1769480 | tf_op jit(solution)/shard_map/ppermute | solution.py:19
  270.9 5.9 %copy-start.8 = (f32[64,3,6,1,128]{4,0,3,2,1:T(8,128)}, f32[64,3,6,1,128]{4,0,3,2,1:T(8,128)S(1)}, u32[]{:S(2)}) copy-start(f32[64,3,6,1,128]{4,0,3,2,1:T(8,128)S(1)} %collective-permute-done.8) | copy-start | bytes 1769476
  276.9 0.8 copy-start.9
  284.9 9.4 %collective-permute-start.10 = (f32[64,3,6,6,1]{0,3,4,2,1:T(8,128)S(1)}, f32[64,3,6,6,1]{0,3,4,2,1:T(8,128)S(1)}, u32[]{:S(2)}, u32[]{:S(2)}) collective-permute-start(f32[64,3,6,6,1]{0,3,4,2,1:T(8,128)S(1)} %copy.82), channel_id=1, source_target_pairs={{0,1},{1,2},{2,3},{4,5},{5,6},{6,7},{8,9},{9,10},{10,11},{12,13},{... | collective-permute-start | bytes 82952 | tf_op jit(solution)/shard_map/ppermute | solution.py:17
  292.8 5.4 %collective-permute-start.11 = (f32[64,3,6,6,1]{0,3,4,2,1:T(8,128)}, f32[64,3,6,6,1]{0,3,4,2,1:T(8,128)}, u32[]{:S(2)}, u32[]{:S(2)}) collective-permute-start(f32[64,3,6,6,1]{0,3,4,2,1:T(8,128)} %copy.84), channel_id=1, source_target_pairs={{1,0},{2,1},{3,2},{5,4},{6,5},{7,6},{9,8},{10,9},{11,10},{13,12},{... | collective-permute-start | bytes 82952 | tf_op jit(solution)/shard_map/ppermute | solution.py:19
  296.8 4.6 %copy-start.6 = (f32[64,3,4,4,128]{4,0,3,2,1:T(8,128)S(1)}, f32[64,3,4,4,128]{4,0,3,2,1:T(8,128)}, u32[]{:S(2)}) copy-start(f32[64,3,4,4,128]{4,0,3,2,1:T(8,128)} %copy-done.5) | copy-start | bytes 4718596
  296.8 4.6 %copy-start.15 = (pred[128]{0:T(512)(128)(4,1)S(1)}, pred[128]{0:T(512)(128)(4,1)}, u32[]{:S(2)}) copy-start(pred[128]{0:T(512)(128)(4,1)} %get-tuple-element.87) | copy-start | bytes 388
Sparse Core Ops, SparseCore 0:
  90.7 136.1 all-reduce.1
where the time goes:
time: 321 us; the launch traced here: 316 us
  waiting for transfers between devices  165 us (51%)
  local copies, waits for them, and re-layouts  58.4 us (18%)
  starting transfers between devices  41.7 us (13%)
  matrix products  20.3 us (6%)
  between operations  14.4 us (4%)
  other arithmetic  14 us (4%)
    psum x1, waiting for transfers between devices, per_device(): coarse_residual = lax.psum(local_coarse, ('gy', 'gz'))  123 us
    ppermute x6, starting transfers between devices, padded_2(): lax.ppermute(tail, axis, [(i, (i + 1) % count) for i in range(ends)])  28.5 us
    ppermute x6, waiting for transfers between devices, padded_2(): lax.ppermute(head, axis, [((i + 1) % count, i) for i in range(ends)])  23.9 us
    ppermute x6, waiting for transfers between devices, padded_2(): lax.ppermute(tail, axis, [(i, (i + 1) % count) for i in range(ends)])  17.7 us
    unnamed x45, local copies, waits for them, and re-layouts  17.5 us
    slice x6, local copies, waits for them, and re-layouts, padded_2(): lax.slice_in_dim(cells, cells.shape[dim] - width, cells.shape[dim], axis=...  14 us
    ppermute x6, starting transfers between devices, padded_2(): lax.ppermute(head, axis, [((i + 1) % count, i) for i in range(ends)])  13.3 us
    dot_general x2, matrix products, add_slot(): jnp.einsum('bij,sbj->sbi', tile_now, chosen, preferred_element_type=jnp.f...  8.45 us
  transfers between devices with their start and end apart: 13, of which 10 were waited for; matrix products, arithmetic and copies ran while one was open for 12% of the time, Pallas kernels for 0%

commit v1 on v0

v1 whole, which is shorter than its diff:
```python
import functools
import math

import jax
import jax.numpy as jnp
from jax import lax
from jax.experimental import pallas as pl
from jax.experimental.pallas import tpu as pltpu
from jax.sharding import PartitionSpec as P

MESH = pl.DeviceIdType.MESH
CHUNKS = 2
GROUP_Y = 4
GROUP_Z = 4
SLOTS = GROUP_Y * GROUP_Z
NEAR = tuple((a, b) for a in range(2) for b in range(GROUP_Z) if (a, b) != (0, 0))
FULL = tuple((a, b) for a in range(GROUP_Y) for b in range(GROUP_Z) if (a, b) != (0, 0))
BF16 = jnp.bfloat16
F32 = jnp.float32
NT = (((1,), (1,)), ((), ()))


def flipped(gy, a):
    return (gy, gy + 1 - 2 * (gy % 2), (gy + 2) % 4, 3 - gy)[a]


def kernel(
    sizes,
    res_hbm,
    scale_hbm,
    basis_hbm,
    index_smem,
    index_hbm,
    inverse_hbm,
    tiles_hbm,
    cols_smem,
    count_smem,
    region_smem,
    visc_smem,
    out_hbm,
    lin,
    scale,
    basis,
    inverse,
    tiles,
    index_all,
    field,
    weighted,
    corr,
    zpack,
    x_low,
    x_high,
    y_low,
    y_high,
    z_low,
    z_high,
    parts,
    part_own,
    picked_rows,
    split_rows,
    gathered,
    load_sem,
    in_sem,
    out_sem,
    face_send,
    face_recv,
    index_send,
    index_recv,
    part_send,
    part_recv,
):
    n_gx, n_gy, n_gz, rhs, blocks, comps, slots = sizes
    rows = rhs // CHUNKS
    gx, gy, gz = lax.axis_index("gx"), lax.axis_index("gy"), lax.axis_index("gz")

    sides = (
        (gx > 0, (gx - 1, gy, gz)),
        (gx < n_gx - 1, (gx + 1, gy, gz)),
        (gy > 0, (gx, gy - 1, gz)),
        (gy < n_gy - 1, (gx, gy + 1, gz)),
        (gz > 0, (gx, gy, gz - 1)),
        (gz < n_gz - 1, (gx, gy, gz + 1)),
    )

    def peer(a, b):
        return (gx, flipped(gy, a), (gz + b) % GROUP_Z)

    def load_chunk(c):
        span = pl.ds(c * rows * blocks, rows * blocks)
        return pltpu.make_async_copy(res_hbm.at[span], lin.at[span], in_sem.at[c])

    loads = (
        pltpu.make_async_copy(index_hbm, index_all.at[0], load_sem.at[0]),
        pltpu.make_async_copy(scale_hbm, scale, load_sem.at[1]),
        pltpu.make_async_copy(inverse_hbm, inverse, load_sem.at[2]),
        pltpu.make_async_copy(basis_hbm, basis, load_sem.at[3]),
        pltpu.make_async_copy(tiles_hbm, tiles, load_sem.at[4]),
    )
    for c in range(CHUNKS):
        load_chunk(c).start()
    for copy in loads:
        copy.start()

    barrier = pltpu.get_barrier_semaphore()
    expected = 0
    for there, device in sides:

        @pl.when(there)
        def _():
            pl.semaphore_signal(barrier, inc=1, device_id=device, device_id_type=MESH)

        expected = expected + there.astype(jnp.int32)
    for a, b in FULL:
        pl.semaphore_signal(barrier, inc=1, device_id=peer(a, b), device_id_type=MESH)
    pl.semaphore_wait(barrier, expected + len(FULL))

    loads[0].wait()

    def index_copy(a, b):
        k = a * GROUP_Z + b
        return pltpu.make_async_remote_copy(
            src_ref=index_all.at[0],
            dst_ref=index_all.at[k],
            send_sem=index_send.at[k],
            recv_sem=index_recv.at[k],
            device_id=peer(a, b),
            device_id_type=MESH,
        )

    for a, b in FULL:
        index_copy(a, b).start()

    lane = lax.broadcasted_iota(jnp.int32, (rows, 128), 1)

    def face_copies(phase, source, c):
        pairs = (
            (source.at[c, :, 0], x_high),
            (source.at[c, :, 3], x_low),
            (source.at[c, :, :, 0], y_high),
            (source.at[c, :, :, 3], y_low),
            (zpack.at[phase, c], z_high),
            (zpack.at[phase, c], z_low),
        )
        return [
            pltpu.make_async_remote_copy(
                src_ref=src,
                dst_ref=dst.at[phase, c],
                send_sem=face_send.at[phase, c, side],
                recv_sem=face_recv.at[phase, c, side ^ 1],
                device_id=sides[side][1],
                device_id_type=MESH,
            )
            for side, (src, dst) in enumerate(pairs)
        ]

    landing = (x_low, x_high, y_low, y_high, z_low, z_high)

    def send_faces(phase, source, c):
        for side, copy in enumerate(face_copies(phase, source, c)):

            @pl.when(sides[side][0])
            def _():
                copy.start()

    def await_faces(phase, source, c):
        for side, copy in enumerate(face_copies(phase, source, c)):
            land = landing[side].at[phase, c]
            arrived = pltpu.make_async_remote_copy(
                src_ref=land,
                dst_ref=land,
                send_sem=face_send.at[phase, c, side],
                recv_sem=face_recv.at[phase, c, side],
                device_id=sides[side][1],
                device_id_type=MESH,
            )

            @pl.when(sides[side][0])
            def _():
                arrived.wait_recv()

    def drain_faces(phase, source, c):
        for side, copy in enumerate(face_copies(phase, source, c)):

            @pl.when(sides[side][0])
            def _():
                copy.wait_send()

    for side in range(6):

        @pl.when(jnp.logical_not(sides[side][0]))
        def _():
            landing[side][...] = jnp.zeros_like(landing[side])

    def packed(acc, value, b):
        return jnp.where(lane // 2 == b, pltpu.roll(value, 2 * b + 1, 1), acc)

    def pack_first(c):
        def body(comp, acc):
            for x in range(4):
                for y in range(4):
                    b = comp * 16 + x * 4 + y
                    value = lin[pl.ds(c * rows * blocks + b, rows, stride=blocks), :]
                    field[c, comp, x, y] = value
                    acc = packed(acc, value, b)
            return acc

        zpack[0, c] = lax.fori_loop(0, comps, body, jnp.zeros((rows, 128), F32))

    def interface_sum(phase, source, c, emit):
        low = pltpu.roll(z_low[phase, c], 1, 1)
        high = pltpu.roll(z_high[phase, c], 127, 1)
        ends = jnp.where(lane % 2 == 1, low, high)
        edge = (lane == 0) | (lane == 127)

        def body(comp, carry):
            for x in range(4):
                for y in range(4):
                    b = comp * 16 + x * 4 + y
                    total = source[c, comp, x, y]
                    total = total + jnp.where(edge, pltpu.roll(ends, 127 - 2 * b, 1), 0.0)
                    if x == 0:
                        total = total + x_low[phase, c, comp, y]
                    if x == 3:
                        total = total + x_high[phase, c, comp, y]
                    if y == 0:
                        total = total + y_low[phase, c, comp, x]
                    if y == 3:
                        total = total + y_high[phase, c, comp, x]
                    emit(b, total * scale[pl.ds(b, 1), :])
            return carry

        lax.fori_loop(0, comps, body, 0)

    for c in range(CHUNKS):
        load_chunk(c).wait()
        pack_first(c)
        send_faces(0, field, c)

    loads[2].wait()

    def pick_row(p, carry):
        picked_rows[pl.ds(p, 1), :] = inverse[pl.ds(index_smem[p], 1), :]
        return carry

    lax.fori_loop(0, 128, pick_row, 0, unroll=8)
    rows_f32 = picked_rows[...]
    high_part = rows_f32.astype(BF16)
    split_rows[0:128, :] = high_part
    split_rows[128:256, :] = (rows_f32 - high_part.astype(F32)).astype(BF16)

    for a, b in FULL:
        index_copy(a, b).wait_recv()

    def pick_columns(k, carry):
        coarse = split_rows.shape[1]
        ids = lax.broadcasted_iota(jnp.int32, (coarse, 128), 0)
        one_hot = jnp.where(ids == index_all[k], 1.0, 0.0).astype(BF16)
        found = jnp.dot(split_rows[...], one_hot, preferred_element_type=F32).astype(BF16)
        gathered[k] = found
        return carry

    lax.fori_loop(0, SLOTS, pick_columns, 0)

    def part_copy(c, a, b, forward):
        slot = (a + 2) * GROUP_Z + b if forward else a * GROUP_Z + b
        return pltpu.make_async_remote_copy(
            src_ref=parts.at[c, 2 * GROUP_Z] if forward else part_own.at[c],
            dst_ref=parts.at[c, slot],
            send_sem=part_send.at[c, slot],
            recv_sem=part_recv.at[c, slot],
            device_id=peer(a, b),
            device_id_type=MESH,
        )

    loads[1].wait()
    loads[3].wait()
    visc = jnp.full((rows, 128), visc_smem[region_smem[0]], F32)
    inv_visc = 1.0 / visc
    coarse_scale = math.sqrt(blocks * 128 / 128)

    for c in range(CHUNKS):
        await_faces(0, field, c)

        def keep(b, value):
            weighted[c, b] = value.astype(BF16)

        interface_sum(0, field, c, keep)
        weighted[c, blocks] = jnp.zeros((rows, 128), BF16)

        def restrict(comp, acc):
            lhs = jnp.concatenate([weighted[c, comp * 16 + j] for j in range(16)], axis=1)
            rhs_part = basis[:, pl.ds(pl.multiple_of(comp * 2048, 2048), 2048)]
            return acc + lax.dot_general(lhs, rhs_part, NT, preferred_element_type=F32)

        part = lax.fori_loop(0, comps, restrict, jnp.zeros((rows, 128), F32))
        part_own[c] = part
        parts[c, 0] = part
        part_copy(c, 2, 0, False).start()
        for a, b in NEAR:
            part_copy(c, a, b, False).start()

        if c == 0:
            loads[4].wait()

        def schur_row(r, carry):
            picks = [
                weighted[c, jnp.where(k < count_smem[r], cols_smem[r * slots + k], blocks)]
                for k in range(slots)
            ]
            lhs = jnp.concatenate(picks, axis=1)
            tile = jnp.concatenate([tiles[r, k] for k in range(slots)], axis=1)
            product = lax.dot_general(lhs, tile, NT, preferred_element_type=F32)
            corr[c, r // 16, (r // 4) % 4, r % 4] = product * inv_visc
            return carry

        lax.fori_loop(0, 12, schur_row, 0, unroll=2)
        part_copy(c, 2, 0, False).wait_recv()
        for a, b in NEAR:
            part_copy(c, a, b, True).start()
        lax.fori_loop(12, blocks, schur_row, 0, unroll=2)
        for a, b in NEAR:
            part_copy(c, a, b, False).wait_recv()
            part_copy(c, a, b, True).wait_recv()

        everyone = jnp.concatenate([parts[c, k] for k in range(SLOTS)], axis=1)
        top = everyone.astype(BF16)
        rest = (everyone - top.astype(F32)).astype(BF16)
        inv_high = jnp.concatenate([gathered[k, 0:128] for k in range(SLOTS)], axis=1)
        inv_low = jnp.concatenate([gathered[k, 128:256] for k in range(SLOTS)], axis=1)
        local = lax.dot_general(top, inv_high, NT, preferred_element_type=F32)
        local = local + lax.dot_general(rest, inv_high, NT, preferred_element_type=F32)
        local = local + lax.dot_general(top, inv_low, NT, preferred_element_type=F32)
        local = local.astype(BF16)

        def prolong(comp, acc):
            rhs_part = basis[:, pl.ds(pl.multiple_of(comp * 2048, 2048), 2048)]
            fix = jnp.dot(local, rhs_part, preferred_element_type=F32) * coarse_scale
            for x in range(4):
                for y in range(4):
                    j = x * 4 + y
                    value = corr[c, comp, x, y] + fix[:, j * 128 : (j + 1) * 128]
                    corr[c, comp, x, y] = value
                    acc = packed(acc, value, comp * 16 + j)
            return acc

        zpack[1, c] = lax.fori_loop(0, comps, prolong, jnp.zeros((rows, 128), F32))
        send_faces(1, corr, c)

    def store_chunk(c):
        span = pl.ds(c * rows * blocks, rows * blocks)
        return pltpu.make_async_copy(lin.at[span], out_hbm.at[span], out_sem.at[c])

    for c in range(CHUNKS):
        await_faces(1, corr, c)

        def emit(b, value):
            lin[pl.ds(c * rows * blocks + b, rows, stride=blocks), :] = value

        interface_sum(1, corr, c, emit)
        store_chunk(c).start()

    for c in range(CHUNKS):
        drain_faces(0, field, c)
        drain_faces(1, corr, c)
        part_copy(c, 2, 0, False).wait_send()
        for a, b in NEAR:
            part_copy(c, a, b, False).wait_send()
            part_copy(c, a, b, True).wait_send()
        store_chunk(c).wait()
    for a, b in FULL:
        index_copy(a, b).wait_send()


def per_device(
    residual,
    interface_scaling,
    primal_basis,
    primal_index,
    coarse_inverse,
    schur_tiles,
    tile_cols,
    tile_count,
    region_id,
    region_viscosity,
):
    rhs, comps, cells_x, cells_y, cells_z = residual.shape
    blocks = comps * cells_x * cells_y
    slots = schur_tiles.shape[4]
    primal = primal_basis.shape[3]
    coarse = coarse_inverse.shape[1]
    rows = rhs // CHUNKS
    sizes = (
        lax.axis_size("gx"),
        lax.axis_size("gy"),
        lax.axis_size("gz"),
        rhs,
        blocks,
        comps,
        slots,
    )
    face = pltpu.VMEM((2, CHUNKS, comps, cells_x, rows, cells_z), F32)
    ends = pltpu.VMEM((2, CHUNKS, rows, cells_z), F32)
    dma = pltpu.SemaphoreType.DMA
    hbm = pl.BlockSpec(memory_space=pl.ANY)
    smem = pl.BlockSpec(memory_space=pltpu.SMEM)
    out = pl.pallas_call(
        functools.partial(kernel, sizes),
        out_shape=jax.ShapeDtypeStruct((rhs * blocks, cells_z), F32),
        in_specs=[hbm, hbm, hbm, smem, hbm, hbm, hbm, smem, smem, smem, smem],
        out_specs=hbm,
        scratch_shapes=[
            pltpu.VMEM((rhs * blocks, cells_z), F32),
            pltpu.VMEM((blocks, cells_z), F32),
            pltpu.VMEM((primal, blocks * cells_z), BF16),
            pltpu.VMEM((coarse, coarse), F32),
            pltpu.VMEM((blocks, slots, cells_z, cells_z), BF16),
            pltpu.VMEM((SLOTS, 1, primal), jnp.int32),
            pltpu.VMEM((CHUNKS, comps, cells_x, cells_y, rows, cells_z), F32),
            pltpu.VMEM((CHUNKS, blocks + 1, rows, cells_z), BF16),
            pltpu.VMEM((CHUNKS, comps, cells_x, cells_y, rows, cells_z), F32),
            ends,
            face,
            face,
            face,
            face,
            ends,
            ends,
            pltpu.VMEM((CHUNKS, SLOTS, rows, primal), F32),
            pltpu.VMEM((CHUNKS, rows, primal), F32),
            pltpu.VMEM((primal, coarse), F32),
            pltpu.VMEM((2 * primal, coarse), BF16),
            pltpu.VMEM((SLOTS, 2 * primal, primal), BF16),
            dma((5,)),
            dma((CHUNKS,)),
            dma((CHUNKS,)),
            dma((2, CHUNKS, 6)),
            dma((2, CHUNKS, 6)),
            dma((SLOTS,)),
            dma((SLOTS,)),
            dma((CHUNKS, SLOTS)),
            dma((CHUNKS, SLOTS)),
        ],
        compiler_params=pltpu.CompilerParams(
            collective_id=0, has_side_effects=True, vmem_limit_bytes=52 * 2**20
        ),
    )(
        residual.reshape(rhs * blocks, cells_z),
        interface_scaling.reshape(blocks, cells_z),
        primal_basis.reshape(primal, blocks * cells_z),
        primal_index.reshape(primal),
        primal_index.reshape(1, primal),
        coarse_inverse,
        schur_tiles.reshape(blocks, slots, cells_z, cells_z),
        tile_cols.reshape(blocks * slots),
        tile_count.reshape(blocks),
        region_id.reshape(1),
        region_viscosity,
    )
    return out.reshape(residual.shape)


def solution(mesh):
    in_specs = (
        P(None, None, "gx", "gy", "gz"),
        P(None, "gx", "gy", "gz"),
        P("gx", "gy", "gz", None, None),
        P("gx", "gy", "gz", None),
        P("gx", None),
        P("gx", "gy", "gz", None, None, None, None),
        P("gx", "gy", "gz", None, None),
        P("gx", "gy", "gz", None),
        P("gx", "gy", "gz"),
        P(),
    )
    out_specs = P(None, None, "gx", "gy", "gz")
    return jax.shard_map(
        per_device, mesh=mesh, in_specs=in_specs, out_specs=out_specs, check_vma=False
    )
```

time: 321 us -> 75 us (0.23); the launches traced: 316 us -> 74.8 us
  waiting for transfers between devices: 165 us -> 0 us
  Pallas kernels: 0 us -> 69.3 us
  local copies, waits for them, and re-layouts: 58.4 us -> 4.73 us
  starting transfers between devices: 41.7 us -> 0 us
  matrix products: 20.3 us -> 0 us
  other arithmetic: 14 us -> 0 us
  between operations: 14.4 us -> 0.67 us
    psum x1 -> x0, waiting for transfers between devices: 123 us -> none  [per_device(): coarse_residual = lax.psum(local_coarse, ('gy', 'gz'))]
    pallas_call x0 -> x1, Pallas kernels: none -> 69.3 us  [per_device(): pl.pallas_call(functools.partial(kernel, sizes), out_shape=jax.ShapeDtype...]
    ppermute x12 -> x0, starting transfers between devices: 41.7 us -> none  [the longest x6 28.5 us: padded_2(): lax.ppermute(tail, axis, [(i, (i + 1) % count) for i in range(ends)])]
    ppermute x12 -> x0, waiting for transfers between devices: 41.7 us -> none  [the longest x6 23.9 us: padded_2(): lax.ppermute(head, axis, [((i + 1) % count, i) for i in range(ends)])]
    slice x10 -> x0, local copies, waits for them, and re-layouts: 20.4 us -> none  [the longest x6 14 us: padded_2(): lax.slice_in_dim(cells, cells.shape[dim] - width, cells.shape[dim], axis=...]
    dot_general x7 -> x0, matrix products: 20.3 us -> none  [the longest x2 8.45 us: add_slot(): jnp.einsum('bij,sbj->sbi', tile_now, chosen, preferred_element_type=jnp.f...]
    unnamed x45 -> x10, local copies, waits for them, and re-layouts: 17.5 us -> 4.61 us
    ppermute x4 -> x0, local copies, waits for them, and re-layouts: 10.6 us -> none  [the longest x2 5.7 us: padded_2(): lax.ppermute(head, axis, [((i + 1) % count, i) for i in range(ends)])]
  transfers between devices with their start and end apart: 13 -> 0, of which waited for: 10 -> 0; matrix products, arithmetic and copies ran while one was open for 12% -> 0% of each run, Pallas kernels for 0% -> 0%
where the time goes in v1:
time: 75 us; the launch traced here: 74.8 us
  Pallas kernels  69.3 us (92%)
  local copies, waits for them, and re-layouts  4.73 us (6%)
    pallas_call x1, Pallas kernels, per_device(): pl.pallas_call(functools.partial(kernel, sizes), out_shape=jax.ShapeDtype...  69.3 us
    unnamed x10, local copies, waits for them, and re-layouts  4.61 us

profile of v1, /device:TPU:97, one launch (start us, length us, event | category | flops | bytes accessed | tf_op | source)
XLA Modules:
  0.0 74.8 jit_solution(9639032699546396910)
XLA Ops:
  0.7 0.8 %copy.11 = s32[1,1,1,48,6]{4,3,2,1,0:T(8,128)S(1)} copy(s32[1,1,1,48,6]{3,2,4,1,0:T(1,128)} %param.16) | data formatting | bytes 2304 | tf_op args[6]
  1.4 0.1 reshape.36.cols_smem
  1.5 0.0 copy-start
  1.6 0.7 copy-done
  2.3 0.0 copy-start.1
  2.3 0.7 copy-done.1
  2.9 0.0 copy-start.2
  2.9 0.7 copy-done.2
  3.6 0.0 copy-start.3
  3.6 0.7 copy-done.3
  4.3 69.3 %shard_map.100 = f32[3072,128]{1,0:T(8,128)S(1)} custom-call(f32[3072,128]{1,0:T(8,128)} %bitcast.18, f32[48,128]{1,0:T(8,128)S(1)} %bitcast.13, bf16[128,6144]{1,0:T(8,128)(2,1)} %bitcast.19, s32[128]{0:T(128)S(1)} %bitcast.14, s32[1,128]{1,0:T(1,128)S(1)} %bitcast.15, f32[1024,1024]{1,0:T(8,128)} %inverse_hbm.1, bf16[48,6,128,128]{3,2,1,0:T(8,128)(2,1)} %bitcast.17, ...), custom_call_target="tpu_custom_call" | custom-call | tf_op jit(solution)/shard_map/pallas_call | solution.py:406
  73.6 1.1 %copy.14 = f32[64,3,4,4,128]{4,3,2,1,0:T(4,128)} copy(f32[64,3,4,4,128]{4,3,2,1,0:T(4,128)S(1)} %bitcast.12) | data formatting | bytes 3145728
Async XLA Ops:
  1.5 0.7 copy-start
  2.3 0.7 copy-start.1
  2.9 0.7 copy-start.2
  3.6 0.7 copy-start.3

commit v2 on v1

--- a/solution.py
+++ b/solution.py
@@ -10,6 +10,9 @@
 
 MESH = pl.DeviceIdType.MESH
 CHUNKS = 2
+ALL = (0, 1, 2, 3, 4, 5)
+AHEAD = (2, 3, 4, 5)
+HELD = (0, 1)
 GROUP_Y = 4
 GROUP_Z = 4
 SLOTS = GROUP_Y * GROUP_Z
@@ -29,15 +32,18 @@
     res_hbm,
     scale_hbm,
     basis_hbm,
-    index_smem,
     index_hbm,
     inverse_hbm,
     tiles_hbm,
+    cols_hbm,
+    count_hbm,
+    region_smem,
+    visc_hbm,
+    out_hbm,
+    index_smem,
     cols_smem,
     count_smem,
-    region_smem,
     visc_smem,
-    out_hbm,
     lin,
     scale,
     basis,
@@ -95,10 +101,17 @@
         pltpu.make_async_copy(inverse_hbm, inverse, load_sem.at[2]),
         pltpu.make_async_copy(basis_hbm, basis, load_sem.at[3]),
         pltpu.make_async_copy(tiles_hbm, tiles, load_sem.at[4]),
+        pltpu.make_async_copy(index_hbm, index_smem, load_sem.at[5]),
+        pltpu.make_async_copy(cols_hbm, cols_smem, load_sem.at[6]),
+        pltpu.make_async_copy(count_hbm, count_smem, load_sem.at[7]),
+        pltpu.make_async_copy(visc_hbm, visc_smem, load_sem.at[8]),
     )
+    loads[0].start()
     for c in range(CHUNKS):
         load_chunk(c).start()
-    for copy in loads:
+    for copy in loads[5:]:
+        copy.start()
+    for copy in loads[1:5]:
         copy.start()
 
     barrier = pltpu.get_barrier_semaphore()
@@ -155,8 +168,10 @@
 
     landing = (x_low, x_high, y_low, y_high, z_low, z_high)
 
-    def send_faces(phase, source, c):
+    def send_faces(phase, source, c, chosen=tuple(range(6))):
         for side, copy in enumerate(face_copies(phase, source, c)):
+            if side not in chosen:
+                continue
 
             @pl.when(sides[side][0])
             def _():
@@ -234,12 +249,15 @@
     for c in range(CHUNKS):
         load_chunk(c).wait()
         pack_first(c)
-        send_faces(0, field, c)
+        send_faces(0, field, c, AHEAD if c else ALL)
+
+    for copy in loads[5:]:
+        copy.wait()
 
     loads[2].wait()
 
     def pick_row(p, carry):
-        picked_rows[pl.ds(p, 1), :] = inverse[pl.ds(index_smem[p], 1), :]
+        picked_rows[pl.ds(p, 1), :] = inverse[pl.ds(index_smem[0, p], 1), :]
         return carry
 
     lax.fori_loop(0, 128, pick_row, 0, unroll=8)
@@ -274,7 +292,7 @@
 
     loads[1].wait()
     loads[3].wait()
-    visc = jnp.full((rows, 128), visc_smem[region_smem[0]], F32)
+    visc = jnp.full((rows, 128), visc_smem[0, region_smem[0, 0, 0]], F32)
     inv_visc = 1.0 / visc
     coarse_scale = math.sqrt(blocks * 128 / 128)
 
@@ -298,13 +316,16 @@
         part_copy(c, 2, 0, False).start()
         for a, b in NEAR:
             part_copy(c, a, b, False).start()
-
+        if c > 0:
+            send_faces(1, corr, c - 1, HELD)
+        if c + 1 < CHUNKS:
+            send_faces(0, field, c + 1, HELD)
         if c == 0:
             loads[4].wait()
 
         def schur_row(r, carry):
             picks = [
-                weighted[c, jnp.where(k < count_smem[r], cols_smem[r * slots + k], blocks)]
+                weighted[c, jnp.where(k < count_smem[0, r], cols_smem[k, 0, r], blocks)]
                 for k in range(slots)
             ]
             lhs = jnp.concatenate(picks, axis=1)
@@ -344,7 +365,7 @@
             return acc
 
         zpack[1, c] = lax.fori_loop(0, comps, prolong, jnp.zeros((rows, 128), F32))
-        send_faces(1, corr, c)
+        send_faces(1, corr, c, AHEAD if c + 1 < CHUNKS else ALL)
 
     def store_chunk(c):
         span = pl.ds(c * rows * blocks, rows * blocks)
@@ -401,14 +422,17 @@
     face = pltpu.VMEM((2, CHUNKS, comps, cells_x, rows, cells_z), F32)
     ends = pltpu.VMEM((2, CHUNKS, rows, cells_z), F32)
     dma = pltpu.SemaphoreType.DMA
-    hbm = pl.BlockSpec(memory_space=pl.ANY)
-    smem = pl.BlockSpec(memory_space=pltpu.SMEM)
+    hbm = pl.BlockSpec(memory_space=pltpu.HBM)
     out = pl.pallas_call(
         functools.partial(kernel, sizes),
         out_shape=jax.ShapeDtypeStruct((rhs * blocks, cells_z), F32),
-        in_specs=[hbm, hbm, hbm, smem, hbm, hbm, hbm, smem, smem, smem, smem],
+        in_specs=[hbm] * 8 + [pl.BlockSpec(memory_space=pltpu.SMEM), hbm],
         out_specs=hbm,
         scratch_shapes=[
+            pltpu.SMEM((1, primal), jnp.int32),
+            pltpu.SMEM((slots, 1, blocks), jnp.int32),
+            pltpu.SMEM((1, blocks), jnp.int32),
+            pltpu.SMEM((1, region_viscosity.shape[0]), F32),
             pltpu.VMEM((rhs * blocks, cells_z), F32),
             pltpu.VMEM((blocks, cells_z), F32),
             pltpu.VMEM((primal, blocks * cells_z), BF16),
@@ -430,7 +454,7 @@
             pltpu.VMEM((primal, coarse), F32),
             pltpu.VMEM((2 * primal, coarse), BF16),
             pltpu.VMEM((SLOTS, 2 * primal, primal), BF16),
-            dma((5,)),
+            dma((9,)),
             dma((CHUNKS,)),
             dma((CHUNKS,)),
             dma((2, CHUNKS, 6)),
@@ -441,20 +465,19 @@
             dma((CHUNKS, SLOTS)),
         ],
         compiler_params=pltpu.CompilerParams(
-            collective_id=0, has_side_effects=True, vmem_limit_bytes=52 * 2**20
+            collective_id=0, has_side_effects=True, vmem_limit_bytes=60 * 2**20
         ),
     )(
         residual.reshape(rhs * blocks, cells_z),
         interface_scaling.reshape(blocks, cells_z),
         primal_basis.reshape(primal, blocks * cells_z),
-        primal_index.reshape(primal),
         primal_index.reshape(1, primal),
         coarse_inverse,
         schur_tiles.reshape(blocks, slots, cells_z, cells_z),
-        tile_cols.reshape(blocks * slots),
-        tile_count.reshape(blocks),
-        region_id.reshape(1),
-        region_viscosity,
+        tile_cols.transpose(0, 1, 4, 2, 3).reshape(slots, 1, blocks),
+        tile_count.reshape(1, blocks),
+        region_id,
+        region_viscosity.reshape(1, -1),
     )
     return out.reshape(residual.shape)
 

time: 75 us -> 60.4 us (0.81)
  Pallas kernels: 69.3 us -> 56.8 us
  local copies, waits for them, and re-layouts: 4.73 us -> 2.82 us
    pallas_call x1, Pallas kernels: 69.3 us -> 56.8 us  [per_device(): pl.pallas_call(functools.partial(kernel, sizes), out_shape=jax.ShapeDtype...]
    unnamed x10 -> x1, local copies, waits for them, and re-layouts: 4.61 us -> 2.82 us
where the time goes in v2:
time: 60.4 us; the launch traced here: 60.3 us
  Pallas kernels  56.8 us (94%)
  local copies, waits for them, and re-layouts  2.82 us (5%)
  between operations  0.66 us (1%)
    pallas_call x1, Pallas kernels, per_device(): pl.pallas_call(functools.partial(kernel, sizes), out_shape=jax.ShapeDtype...  56.8 us
    unnamed x1, local copies, waits for them, and re-layouts  2.82 us

profile of v2, /device:TPU:97, one launch (start us, length us, event | category | flops | bytes accessed | tf_op | source)
XLA Modules:
  0.0 60.3 jit_solution(5223505703467312747)
XLA Ops:
  0.7 56.8 %shard_map.100 = f32[3072,128]{1,0:T(8,128)} custom-call(f32[3072,128]{1,0:T(8,128)} %bitcast.13, f32[48,128]{1,0:T(8,128)} %bitcast.15, bf16[128,6144]{1,0:T(8,128)(2,1)} %bitcast.14, s32[1,128]{1,0:T(1,128)} %bitcast.17, f32[1024,1024]{1,0:T(8,128)} %inverse_hbm.1, bf16[48,6,128,128]{3,2,1,0:T(8,128)(2,1)} %bitcast.11, s32[6,1,48]{2,1,0:T(1,128)} %bitcast.16, ...), custom_call_target="tpu_custom_call" | custom-call | tf_op jit(solution)/shard_map/pallas_call | solution.py:426
  57.5 2.8 %copy.13 = f32[64,3,4,4,128]{4,3,2,1,0:T(4,128)} copy(f32[64,3,4,4,128]{4,3,2,1,0:T(4,128)} %bitcast.12) | data formatting | bytes 3145728

commit v3 on v2

--- a/solution.py
+++ b/solution.py
@@ -106,12 +106,10 @@
         pltpu.make_async_copy(count_hbm, count_smem, load_sem.at[7]),
         pltpu.make_async_copy(visc_hbm, visc_smem, load_sem.at[8]),
     )
-    loads[0].start()
     for c in range(CHUNKS):
         load_chunk(c).start()
+    loads[0].start()
     for copy in loads[5:]:
-        copy.start()
-    for copy in loads[1:5]:
         copy.start()
 
     barrier = pltpu.get_barrier_semaphore()
@@ -125,9 +123,6 @@
         expected = expected + there.astype(jnp.int32)
     for a, b in FULL:
         pl.semaphore_signal(barrier, inc=1, device_id=peer(a, b), device_id_type=MESH)
-    pl.semaphore_wait(barrier, expected + len(FULL))
-
-    loads[0].wait()
 
     def index_copy(a, b):
         k = a * GROUP_Z + b
@@ -139,9 +134,6 @@
             device_id=peer(a, b),
             device_id_type=MESH,
         )
-
-    for a, b in FULL:
-        index_copy(a, b).start()
 
     lane = lax.broadcasted_iota(jnp.int32, (rows, 128), 1)
 
@@ -200,12 +192,6 @@
             def _():
                 copy.wait_send()
 
-    for side in range(6):
-
-        @pl.when(jnp.logical_not(sides[side][0]))
-        def _():
-            landing[side][...] = jnp.zeros_like(landing[side])
-
     def packed(acc, value, b):
         return jnp.where(lane // 2 == b, pltpu.roll(value, 2 * b + 1, 1), acc)
 
@@ -246,10 +232,28 @@
 
         lax.fori_loop(0, comps, body, 0)
 
-    for c in range(CHUNKS):
+    load_chunk(0).wait()
+    pack_first(0)
+    loads[2].start()
+    loads[0].wait()
+    pl.semaphore_wait(barrier, expected + len(FULL))
+    for a, b in FULL:
+        index_copy(a, b).start()
+    send_faces(0, field, 0)
+    for c in range(1, CHUNKS):
         load_chunk(c).wait()
         pack_first(c)
-        send_faces(0, field, c, AHEAD if c else ALL)
+        send_faces(0, field, c, AHEAD)
+
+    for k in (1, 3, 4):
+        loads[k].start()
+
+    for side in range(6):
+
+        @pl.when(jnp.logical_not(sides[side][0]))
+        def _():
+            landing[side][...] = jnp.zeros_like(landing[side])
+
 
     for copy in loads[5:]:
         copy.wait()
@@ -423,6 +427,21 @@
     ends = pltpu.VMEM((2, CHUNKS, rows, cells_z), F32)
     dma = pltpu.SemaphoreType.DMA
     hbm = pl.BlockSpec(memory_space=pltpu.HBM)
+    operands = (
+        residual.reshape(rhs * blocks, cells_z),
+        interface_scaling.reshape(blocks, cells_z),
+        primal_basis.reshape(primal, blocks * cells_z),
+        primal_index.reshape(1, primal),
+        coarse_inverse,
+        schur_tiles.reshape(blocks, slots, cells_z, cells_z),
+        tile_cols.transpose(0, 1, 4, 2, 3).reshape(slots, 1, blocks),
+        tile_count.reshape(1, blocks),
+        region_id,
+        region_viscosity.reshape(1, -1),
+    )
+    operands = [
+        v if v.size == 1 else pltpu.with_memory_space_constraint(v, pltpu.HBM) for v in operands
+    ]
     out = pl.pallas_call(
         functools.partial(kernel, sizes),
         out_shape=jax.ShapeDtypeStruct((rhs * blocks, cells_z), F32),
@@ -465,20 +484,9 @@
             dma((CHUNKS, SLOTS)),
         ],
         compiler_params=pltpu.CompilerParams(
-            collective_id=0, has_side_effects=True, vmem_limit_bytes=60 * 2**20
+            collective_id=0, has_side_effects=True, vmem_limit_bytes=52 * 2**20
         ),
-    )(
-        residual.reshape(rhs * blocks, cells_z),
-        interface_scaling.reshape(blocks, cells_z),
-        primal_basis.reshape(primal, blocks * cells_z),
-        primal_index.reshape(1, primal),
-        coarse_inverse,
-        schur_tiles.reshape(blocks, slots, cells_z, cells_z),
-        tile_cols.transpose(0, 1, 4, 2, 3).reshape(slots, 1, blocks),
-        tile_count.reshape(1, blocks),
-        region_id,
-        region_viscosity.reshape(1, -1),
-    )
+    )(*operands)
     return out.reshape(residual.shape)
 
 

time: 60.4 us -> 57.5 us (0.952)
  local copies, waits for them, and re-layouts: 2.82 us -> 1.15 us
  Pallas kernels: 56.8 us -> 55.6 us
    unnamed x1, local copies, waits for them, and re-layouts: 2.82 us -> 1.15 us
    pallas_call x1, Pallas kernels: 56.8 us -> 55.6 us  [per_device(): pl.pallas_call(functools.partial(kernel, sizes), out_shape=jax.ShapeDtype...]
where the time goes in v3:
time: 57.5 us; the launch traced here: 57.4 us
  Pallas kernels  55.6 us (97%)
  local copies, waits for them, and re-layouts  1.15 us (2%)
  between operations  0.66 us (1%)
    pallas_call x1, Pallas kernels, per_device(): pl.pallas_call(functools.partial(kernel, sizes), out_shape=jax.ShapeDtype...  55.6 us

profile of v3, /device:TPU:97, one launch (start us, length us, event | category | flops | bytes accessed | tf_op | source)
XLA Modules:
  0.0 57.4 jit_solution(15358952430301298457)
XLA Ops:
  0.7 55.6 %shard_map.100 = f32[3072,128]{1,0:T(8,128)S(1)} custom-call(f32[3072,128]{1,0:T(8,128)} %bitcast.13, f32[48,128]{1,0:T(8,128)} %bitcast.15, bf16[128,6144]{1,0:T(8,128)(2,1)} %bitcast.14, s32[1,128]{1,0:T(1,128)} %bitcast.17, f32[1024,1024]{1,0:T(8,128)} %inverse_hbm.1, bf16[48,6,128,128]{3,2,1,0:T(8,128)(2,1)} %bitcast.12, s32[6,1,48]{2,1,0:T(1,128)} %bitcast.16, ...), custom_call_target="tpu_custom_call" | custom-call | tf_op jit(solution)/shard_map/pallas_call | solution.py:445
  56.2 1.1 %copy.13 = f32[64,3,4,4,128]{4,3,2,1,0:T(4,128)} copy(f32[64,3,4,4,128]{4,3,2,1,0:T(4,128)S(1)} %bitcast.11) | data formatting | bytes 3145728

commit v4 on v3

--- a/solution.py
+++ b/solution.py
@@ -10,9 +10,9 @@
 
 MESH = pl.DeviceIdType.MESH
 CHUNKS = 2
-ALL = (0, 1, 2, 3, 4, 5)
-AHEAD = (2, 3, 4, 5)
-HELD = (0, 1)
+AHEAD = 0
+INNER = (1, 2)
+OUTER = (0, 3)
 GROUP_Y = 4
 GROUP_Z = 4
 SLOTS = GROUP_Y * GROUP_Z
@@ -39,7 +39,7 @@
     count_hbm,
     region_smem,
     visc_hbm,
-    out_hbm,
+    out,
     index_smem,
     cols_smem,
     count_smem,
@@ -67,7 +67,6 @@
     gathered,
     load_sem,
     in_sem,
-    out_sem,
     face_send,
     face_recv,
     index_send,
@@ -160,17 +159,33 @@
 
     landing = (x_low, x_high, y_low, y_high, z_low, z_high)
 
-    def send_faces(phase, source, c, chosen=tuple(range(6))):
-        for side, copy in enumerate(face_copies(phase, source, c)):
-            if side not in chosen:
-                continue
+    def x_copy(phase, source, c, side, comp):
+        return pltpu.make_async_remote_copy(
+            src_ref=source.at[c, comp, 3 * side],
+            dst_ref=(x_high, x_low)[side].at[phase, c, comp],
+            send_sem=face_send.at[phase, c, side],
+            recv_sem=face_recv.at[phase, c, 1 - side],
+            device_id=sides[side][1],
+            device_id_type=MESH,
+        )
+
+    def send_faces(phase, source, c):
+        for side in (4, 5, 2, 3):
 
             @pl.when(sides[side][0])
             def _():
-                copy.start()
-
-    def await_faces(phase, source, c):
-        for side, copy in enumerate(face_copies(phase, source, c)):
+                face_copies(phase, source, c)[side].start()
+
+    def send_x(phase, source, c, first, last):
+        for comp in range(first, last):
+            for side in range(2):
+
+                @pl.when(sides[side][0])
+                def _():
+                    x_copy(phase, source, c, side, comp).start()
+
+    def await_faces(phase, c, chosen):
+        for side in chosen:
             land = landing[side].at[phase, c]
             arrived = pltpu.make_async_remote_copy(
                 src_ref=land,
@@ -207,14 +222,14 @@
 
         zpack[0, c] = lax.fori_loop(0, comps, body, jnp.zeros((rows, 128), F32))
 
-    def interface_sum(phase, source, c, emit):
+    def interface_sum(phase, source, c, planes, emit):
         low = pltpu.roll(z_low[phase, c], 1, 1)
         high = pltpu.roll(z_high[phase, c], 127, 1)
         ends = jnp.where(lane % 2 == 1, low, high)
         edge = (lane == 0) | (lane == 127)
 
         def body(comp, carry):
-            for x in range(4):
+            for x in planes:
                 for y in range(4):
                     b = comp * 16 + x * 4 + y
                     total = source[c, comp, x, y]
@@ -240,10 +255,12 @@
     for a, b in FULL:
         index_copy(a, b).start()
     send_faces(0, field, 0)
+    send_x(0, field, 0, 0, comps)
     for c in range(1, CHUNKS):
         load_chunk(c).wait()
         pack_first(c)
-        send_faces(0, field, c, AHEAD)
+        send_faces(0, field, c)
+        send_x(0, field, c, 0, AHEAD)
 
     for k in (1, 3, 4):
         loads[k].start()
@@ -301,29 +318,40 @@
     coarse_scale = math.sqrt(blocks * 128 / 128)
 
     for c in range(CHUNKS):
-        await_faces(0, field, c)
-
         def keep(b, value):
             weighted[c, b] = value.astype(BF16)
 
-        interface_sum(0, field, c, keep)
+        def restrict(planes):
+            def body(comp, acc):
+                picks = [weighted[c, comp * 16 + x * 4 + y] for x in planes for y in range(4)]
+                spans = [
+                    basis[:, pl.ds(pl.multiple_of(comp * 2048 + x * 512, 512), 512)] for x in planes
+                ]
+                return acc + lax.dot_general(
+                    jnp.concatenate(picks, axis=1),
+                    jnp.concatenate(spans, axis=1),
+                    NT,
+                    preferred_element_type=F32,
+                )
+
+            return body
+
+        await_faces(0, c, (2, 3, 4, 5))
+        interface_sum(0, field, c, INNER, keep)
+        part = lax.fori_loop(0, comps, restrict(INNER), jnp.zeros((rows, 128), F32))
+        await_faces(0, c, (0, 1))
+        interface_sum(0, field, c, OUTER, keep)
         weighted[c, blocks] = jnp.zeros((rows, 128), BF16)
-
-        def restrict(comp, acc):
-            lhs = jnp.concatenate([weighted[c, comp * 16 + j] for j in range(16)], axis=1)
-            rhs_part = basis[:, pl.ds(pl.multiple_of(comp * 2048, 2048), 2048)]
-            return acc + lax.dot_general(lhs, rhs_part, NT, preferred_element_type=F32)
-
-        part = lax.fori_loop(0, comps, restrict, jnp.zeros((rows, 128), F32))
+        part = lax.fori_loop(0, comps, restrict(OUTER), part)
         part_own[c] = part
         parts[c, 0] = part
         part_copy(c, 2, 0, False).start()
         for a, b in NEAR:
             part_copy(c, a, b, False).start()
         if c > 0:
-            send_faces(1, corr, c - 1, HELD)
+            send_x(1, corr, c - 1, AHEAD, comps)
         if c + 1 < CHUNKS:
-            send_faces(0, field, c + 1, HELD)
+            send_x(0, field, c + 1, AHEAD, comps)
         if c == 0:
             loads[4].wait()
 
@@ -369,20 +397,18 @@
             return acc
 
         zpack[1, c] = lax.fori_loop(0, comps, prolong, jnp.zeros((rows, 128), F32))
-        send_faces(1, corr, c, AHEAD if c + 1 < CHUNKS else ALL)
-
-    def store_chunk(c):
-        span = pl.ds(c * rows * blocks, rows * blocks)
-        return pltpu.make_async_copy(lin.at[span], out_hbm.at[span], out_sem.at[c])
+        send_faces(1, corr, c)
+        send_x(1, corr, c, 0, AHEAD if c + 1 < CHUNKS else comps)
 
     for c in range(CHUNKS):
-        await_faces(1, corr, c)
 
         def emit(b, value):
-            lin[pl.ds(c * rows * blocks + b, rows, stride=blocks), :] = value
-
-        interface_sum(1, corr, c, emit)
-        store_chunk(c).start()
+            out[pl.ds(c * rows * blocks + b, rows, stride=blocks), :] = value
+
+        await_faces(1, c, (2, 3, 4, 5))
+        interface_sum(1, corr, c, INNER, emit)
+        await_faces(1, c, (0, 1))
+        interface_sum(1, corr, c, OUTER, emit)
 
     for c in range(CHUNKS):
         drain_faces(0, field, c)
@@ -391,7 +417,6 @@
         for a, b in NEAR:
             part_copy(c, a, b, False).wait_send()
             part_copy(c, a, b, True).wait_send()
-        store_chunk(c).wait()
     for a, b in FULL:
         index_copy(a, b).wait_send()
 
@@ -446,7 +471,7 @@
         functools.partial(kernel, sizes),
         out_shape=jax.ShapeDtypeStruct((rhs * blocks, cells_z), F32),
         in_specs=[hbm] * 8 + [pl.BlockSpec(memory_space=pltpu.SMEM), hbm],
-        out_specs=hbm,
+        out_specs=pl.BlockSpec(memory_space=pltpu.VMEM),
         scratch_shapes=[
             pltpu.SMEM((1, primal), jnp.int32),
             pltpu.SMEM((slots, 1, blocks), jnp.int32),
@@ -475,7 +500,6 @@
             pltpu.VMEM((SLOTS, 2 * primal, primal), BF16),
             dma((9,)),
             dma((CHUNKS,)),
-            dma((CHUNKS,)),
             dma((2, CHUNKS, 6)),
             dma((2, CHUNKS, 6)),
             dma((SLOTS,)),

time: 57.5 us -> 56.1 us (0.976); the launches traced: 57.4 us -> 55.4 us
  Pallas kernels: 55.6 us -> 53.6 us
    pallas_call x1, Pallas kernels: 55.6 us -> 53.6 us  [per_device(): pl.pallas_call(functools.partial(kernel, sizes), out_shape=jax.ShapeDtype...]
where the time goes in v4:
time: 56.1 us; the launch traced here: 55.4 us
  Pallas kernels  53.6 us (96%)
  local copies, waits for them, and re-layouts  1.15 us (2%)
  between operations  0.66 us (1%)
    pallas_call x1, Pallas kernels, per_device(): pl.pallas_call(functools.partial(kernel, sizes), out_shape=jax.ShapeDtype...  53.6 us
    unnamed x1, local copies, waits for them, and re-layouts  1.15 us

profile of v4, /device:TPU:97, one launch (start us, length us, event | category | flops | bytes accessed | tf_op | source)
XLA Modules:
  0.0 55.4 jit_solution(17782284889785469075)
XLA Ops:
  0.7 53.6 %shard_map.100 = f32[3072,128]{1,0:T(8,128)S(1)} custom-call(f32[3072,128]{1,0:T(8,128)} %bitcast.13, f32[48,128]{1,0:T(8,128)} %bitcast.15, bf16[128,6144]{1,0:T(8,128)(2,1)} %bitcast.14, s32[1,128]{1,0:T(1,128)} %bitcast.17, f32[1024,1024]{1,0:T(8,128)} %inverse_hbm.1, bf16[48,6,128,128]{3,2,1,0:T(8,128)(2,1)} %bitcast.12, s32[6,1,48]{2,1,0:T(1,128)} %bitcast.16, ...), custom_call_target="tpu_custom_call" | custom-call | tf_op jit(solution)/shard_map/pallas_call | solution.py:470
  54.3 1.1 %copy.13 = f32[64,3,4,4,128]{4,3,2,1,0:T(4,128)} copy(f32[64,3,4,4,128]{4,3,2,1,0:T(4,128)S(1)} %bitcast.11) | data formatting | bytes 3145728

commit v5 on v4

--- a/solution.py
+++ b/solution.py
@@ -10,7 +10,7 @@
 
 MESH = pl.DeviceIdType.MESH
 CHUNKS = 2
-AHEAD = 0
+RELAYED = ((1, 1),)
 INNER = (1, 2)
 OUTER = (0, 3)
 GROUP_Y = 4
@@ -60,6 +60,7 @@
     y_high,
     z_low,
     z_high,
+    relay,
     parts,
     part_own,
     picked_rows,
@@ -73,6 +74,8 @@
     index_recv,
     part_send,
     part_recv,
+    relay_send,
+    relay_recv,
 ):
     n_gx, n_gy, n_gz, rhs, blocks, comps, slots = sizes
     rows = rhs // CHUNKS
@@ -113,7 +116,11 @@
 
     barrier = pltpu.get_barrier_semaphore()
     expected = 0
-    for there, device in sides:
+    two_off = (
+        (gx > 1, (gx - 2, gy, gz)),
+        (gx < n_gx - 2, (gx + 2, gy, gz)),
+    )
+    for there, device in sides + two_off:
 
         @pl.when(there)
         def _():
@@ -159,16 +166,64 @@
 
     landing = (x_low, x_high, y_low, y_high, z_low, z_high)
 
-    def x_copy(phase, source, c, side, comp):
+    odd, level = gx % 2, gx // 2
+    detour = odd * (level + 1) + (1 - odd) * (4 - level)
+    passing = odd * level + (1 - odd) * (3 - level)
+
+    def x_piece(phase, source, c, side, j):
         return pltpu.make_async_remote_copy(
-            src_ref=source.at[c, comp, 3 * side],
-            dst_ref=(x_high, x_low)[side].at[phase, c, comp],
+            src_ref=source.at[c, :, 3 * side, j],
+            dst_ref=(x_high, x_low)[side].at[phase, c, :, j],
             send_sem=face_send.at[phase, c, side],
             recv_sem=face_recv.at[phase, c, 1 - side],
             device_id=sides[side][1],
             device_id_type=MESH,
         )
 
+    def x_detour(phase, source, c, side, j):
+        return pltpu.make_async_remote_copy(
+            src_ref=source.at[c, :, 3 * side, j],
+            dst_ref=relay.at[phase, j],
+            send_sem=face_send.at[phase, c, side],
+            recv_sem=relay_recv.at[phase, j],
+            device_id=two_off[side][1],
+            device_id_type=MESH,
+        )
+
+    def x_onward(phase, c, side, j):
+        return pltpu.make_async_remote_copy(
+            src_ref=relay.at[phase, j],
+            dst_ref=(x_low, x_high)[side].at[phase, c, :, j],
+            send_sem=relay_send.at[phase, j],
+            recv_sem=face_recv.at[phase, c, side],
+            device_id=sides[side][1],
+            device_id_type=MESH,
+        )
+
+    def send_onward(phase, c):
+        for side in range(2):
+            for j in range(3):
+
+                @pl.when((odd == 1 - side) & (j < passing))
+                def _():
+                    pltpu.make_async_remote_copy(
+                        src_ref=relay.at[phase, j],
+                        dst_ref=relay.at[phase, j],
+                        send_sem=relay_send.at[phase, j],
+                        recv_sem=relay_recv.at[phase, j],
+                        device_id=sides[side][1],
+                        device_id_type=MESH,
+                    ).wait_recv()
+                    x_onward(phase, c, side, j).start()
+
+    def drain_onward(phase, c):
+        for side in range(2):
+            for j in range(3):
+
+                @pl.when((odd == 1 - side) & (j < passing))
+                def _():
+                    x_onward(phase, c, side, j).wait_send()
+
     def send_faces(phase, source, c):
         for side in (4, 5, 2, 3):
 
@@ -176,13 +231,27 @@
             def _():
                 face_copies(phase, source, c)[side].start()
 
-    def send_x(phase, source, c, first, last):
-        for comp in range(first, last):
+    def send_x(phase, source, c):
+        copies = face_copies(phase, source, c)
+        relayed = (phase, c) in RELAYED
+        for side in range(2):
+
+            @pl.when(sides[side][0] & (odd != side) if relayed else sides[side][0])
+            def _():
+                copies[side].start()
+
+        if relayed:
             for side in range(2):
-
-                @pl.when(sides[side][0])
-                def _():
-                    x_copy(phase, source, c, side, comp).start()
+                for j in range(4):
+                    if j < 3:
+
+                        @pl.when(sides[side][0] & (odd == side) & (j < detour))
+                        def _():
+                            x_detour(phase, source, c, side, j).start()
+
+                    @pl.when(sides[side][0] & (odd == side) & (j >= detour))
+                    def _():
+                        x_piece(phase, source, c, side, j).start()
 
     def await_faces(phase, c, chosen):
         for side in chosen:
@@ -255,12 +324,11 @@
     for a, b in FULL:
         index_copy(a, b).start()
     send_faces(0, field, 0)
-    send_x(0, field, 0, 0, comps)
+    send_x(0, field, 0)
     for c in range(1, CHUNKS):
         load_chunk(c).wait()
         pack_first(c)
         send_faces(0, field, c)
-        send_x(0, field, c, 0, AHEAD)
 
     for k in (1, 3, 4):
         loads[k].start()
@@ -272,6 +340,8 @@
             landing[side][...] = jnp.zeros_like(landing[side])
 
 
+    if (0, 0) in RELAYED:
+        send_onward(0, 0)
     for copy in loads[5:]:
         copy.wait()
 
@@ -349,9 +419,9 @@
         for a, b in NEAR:
             part_copy(c, a, b, False).start()
         if c > 0:
-            send_x(1, corr, c - 1, AHEAD, comps)
+            send_x(1, corr, c - 1)
         if c + 1 < CHUNKS:
-            send_x(0, field, c + 1, AHEAD, comps)
+            send_x(0, field, c + 1)
         if c == 0:
             loads[4].wait()
 
@@ -398,13 +468,16 @@
 
         zpack[1, c] = lax.fori_loop(0, comps, prolong, jnp.zeros((rows, 128), F32))
         send_faces(1, corr, c)
-        send_x(1, corr, c, 0, AHEAD if c + 1 < CHUNKS else comps)
+        if c + 1 == CHUNKS:
+            send_x(1, corr, c)
 
     for c in range(CHUNKS):
 
         def emit(b, value):
             out[pl.ds(c * rows * blocks + b, rows, stride=blocks), :] = value
 
+        if c == 0 and (1, 1) in RELAYED:
+            send_onward(1, 1)
         await_faces(1, c, (2, 3, 4, 5))
         interface_sum(1, corr, c, INNER, emit)
         await_faces(1, c, (0, 1))
@@ -417,6 +490,8 @@
         for a, b in NEAR:
             part_copy(c, a, b, False).wait_send()
             part_copy(c, a, b, True).wait_send()
+    for phase, c in RELAYED:
+        drain_onward(phase, c)
     for a, b in FULL:
         index_copy(a, b).wait_send()
 
@@ -493,6 +568,7 @@
             face,
             ends,
             ends,
+            pltpu.VMEM((2, 3, comps, rows, cells_z), F32),
             pltpu.VMEM((CHUNKS, SLOTS, rows, primal), F32),
             pltpu.VMEM((CHUNKS, rows, primal), F32),
             pltpu.VMEM((primal, coarse), F32),
@@ -506,6 +582,8 @@
             dma((SLOTS,)),
             dma((CHUNKS, SLOTS)),
             dma((CHUNKS, SLOTS)),
+            dma((2, 3)),
+            dma((2, 3)),
         ],
         compiler_params=pltpu.CompilerParams(
             collective_id=0, has_side_effects=True, vmem_limit_bytes=52 * 2**20

time: 56.1 us -> 55.1 us (0.982)
  Pallas kernels: 53.6 us -> 52.8 us
    pallas_call x1, Pallas kernels: 53.6 us -> 52.8 us  [per_device(): pl.pallas_call(functools.partial(kernel, sizes), out_shape=jax.ShapeDtype...]
where the time goes in v5:
time: 55.1 us; the launch traced here: 54.6 us
  Pallas kernels  52.8 us (96%)
  local copies, waits for them, and re-layouts  1.15 us (2%)
  between operations  0.66 us (1%)
    pallas_call x1, Pallas kernels, per_device(): pl.pallas_call(functools.partial(kernel, sizes), out_shape=jax.ShapeDtype...  52.8 us
    unnamed x1, local copies, waits for them, and re-layouts  1.15 us

profile of v5, /device:TPU:97, one launch (start us, length us, event | category | flops | bytes accessed | tf_op | source)
XLA Modules:
  0.0 54.6 jit_solution(11009484955412515048)
XLA Ops:
  0.7 52.8 %shard_map.100 = f32[3072,128]{1,0:T(8,128)S(1)} custom-call(f32[3072,128]{1,0:T(8,128)} %bitcast.13, f32[48,128]{1,0:T(8,128)} %bitcast.15, bf16[128,6144]{1,0:T(8,128)(2,1)} %bitcast.14, s32[1,128]{1,0:T(1,128)} %bitcast.17, f32[1024,1024]{1,0:T(8,128)} %inverse_hbm.1, bf16[48,6,128,128]{3,2,1,0:T(8,128)(2,1)} %bitcast.12, s32[6,1,48]{2,1,0:T(1,128)} %bitcast.16, ...), custom_call_target="tpu_custom_call" | custom-call | tf_op jit(solution)/shard_map/pallas_call | solution.py:545
  53.4 1.1 %copy.13 = f32[64,3,4,4,128]{4,3,2,1,0:T(4,128)} copy(f32[64,3,4,4,128]{4,3,2,1,0:T(4,128)S(1)} %bitcast.11) | data formatting | bytes 3145728
